TPU v7x, 512 devices: a whole 4x8x8 slice. The times are simulated.
512 devices in a mesh: seq: 64 (over x, y, core), chan: 8 (over z).
Axes of the slice: x: 4, y: 8, z: 8, core: 2. Of those that a mesh axis runs over, the one named last changes fastest.
Arguments:
- gate_outer: bfloat16 [8192, 4096], P('seq', 'chan'), may hold values from -520 to 520
- gate_inner: bfloat16 [8192, 4096], P('seq', 'chan'), may hold values from -6 to 6
- value_in: bfloat16 [8192, 4096], P('seq', 'chan'), may hold values from -6 to 6
- pole_rates: float32 [8, 4096], P(None, 'chan'), may hold values from 0 to 1, as said below
- pole_weights: float32 [8, 4096], P(None, 'chan'), may hold values from -4 to 4
- skip_gain: float32 [4096], P('chan'), may hold values from -1 to 1
- query_rows: bfloat16 [8192, 4096], P('seq', 'chan'), may hold values from -6 to 6
- key_rows: bfloat16 [8192, 4096], P('seq', 'chan'), may hold values from -6 to 6
Outputs:
- mixed: bfloat16 [8192, 4096], P('seq', 'chan')
Inputs may be any that keep to these rules, and one draw needn't show every extreme that they name: `pole_rates`: each rate is positive and at most 1/30.
All inputs are finite; a program needn't handle non-finite values.
Results may differ from a plain program's by a relative error of at most 0.0065.
Values may be sent and summed in bfloat16 or wider, within the bound.
A program may use at most 128 MiB of HBM per device.

v0:
```python
import math
import jax
import jax.numpy as jnp
from jax import lax
from jax.sharding import PartitionSpec as P

HD = 128


def prefix(part, axis, combine, identity):
    place = lax.axis_index(axis)
    gathered = jax.tree.map(lambda a: lax.all_gather(a, axis), part)
    state = jax.tree.map(lambda a, e: jnp.zeros_like(a) + jnp.asarray(e, a.dtype), part, identity)

    def one(turn, state):
        return combine(
            state, jax.tree.map(lambda a: lax.dynamic_index_in_dim(a, turn, 0, False), gathered)
        )

    return lax.fori_loop(0, place, one, state)


def block_update(carried, queries, query_pos, key_part, value_part, key_start, score_scale):
    run_max, run_sum, run_acc = carried
    heads_here = run_max.shape[0]
    key_count = key_part.shape[0]
    query_heads = queries.reshape(queries.shape[0], heads_here, -1)
    key_heads = key_part.reshape(key_count, heads_here, -1)
    value_heads = value_part.reshape(key_count, heads_here, -1)
    scores = (
        jnp.einsum("qhd,khd->hqk", query_heads, key_heads, preferred_element_type=jnp.float32)
        * score_scale
    )
    key_pos = key_start + jnp.arange(key_count, dtype=jnp.int32)
    visible = key_pos[None, None, :] <= query_pos[None, :, None]
    scores = jnp.where(visible, scores, -1e30)
    new_max = jnp.maximum(run_max, jnp.max(scores, axis=2))
    rescale = jnp.exp(run_max - new_max)
    expo = jnp.where(visible, jnp.exp(scores - new_max[:, :, None]), 0.0)
    new_sum = run_sum * rescale + jnp.sum(expo, axis=2)
    new_acc = run_acc * rescale[:, :, None] + jnp.einsum(
        "hqk,khd->hqd", expo.astype(jnp.bfloat16), value_heads, preferred_element_type=jnp.float32
    )
    return (new_max, new_sum, new_acc)


def fold_keys(carried, queries, query_pos, pieces, score_scale):
    key_piece, value_piece = pieces
    count_rows = key_piece.shape[0]
    step_rows = math.gcd(count_rows, 1024)

    def one_step(step_index, current):
        sub_start = step_index * step_rows
        key_part = lax.dynamic_slice_in_dim(key_piece, sub_start, step_rows, 0)
        value_part = lax.dynamic_slice_in_dim(value_piece, sub_start, step_rows, 0)
        return block_update(
            current, queries, query_pos, key_part, value_part, sub_start, score_scale
        )

    return lax.fori_loop(0, count_rows // step_rows, one_step, carried)


def finish(carried):
    run_max, run_sum, run_acc = carried
    normed = run_acc / run_sum[:, :, None]
    heads_here, rows_here, depth = normed.shape
    return (
        jnp.transpose(normed, (1, 0, 2)).reshape(rows_here, heads_here * depth).astype(jnp.bfloat16)
    )


def local(
    gate_outer, gate_inner, value_in, pole_rates, pole_weights, skip_gain, query_rows, key_rows
):
    tok_rows, width = gate_outer.shape
    poles_here = pole_rates.shape[0]
    seq_index = lax.axis_index("seq")
    chan_count = lax.axis_size("chan")
    gated = gate_inner.astype(jnp.float32) * value_in.astype(jnp.float32)
    offsets = jnp.arange(tok_rows, dtype=jnp.float32)
    growth = jnp.exp(offsets[:, None, None] * pole_rates[None, :, :])
    weighted = growth * gated[:, None, :]
    lower = (jnp.arange(tok_rows)[:, None] >= jnp.arange(tok_rows)[None, :]).astype(jnp.float32)
    running = jnp.dot(
        lower, weighted.reshape(tok_rows, poles_here * width), precision=lax.Precision.HIGHEST
    )
    running = running.reshape(tok_rows, poles_here, width)
    block_span = jnp.float32(tok_rows)
    summary = running[-1] * jnp.exp(-(block_span - 1.0) * pole_rates)

    def chain_states(earlier, later):
        fade = jnp.exp(-block_span * later[1] * pole_rates)
        return (later[0] + fade * earlier[0], earlier[1] + later[1])

    identity = (jnp.zeros_like(summary), jnp.zeros((1, 1), jnp.float32))
    carry_in, block_count = prefix(
        (summary, jnp.ones((1, 1), jnp.float32)), "seq", chain_states, identity
    )
    decayed = jnp.exp(-offsets[:, None, None] * pole_rates[None, :, :])
    modal = decayed * (running + (jnp.exp(-pole_rates) * carry_in)[None, :, :])
    filtered = jnp.sum(modal * (pole_weights * jnp.sqrt(pole_rates))[None, :, :], axis=1)
    conv_out = gate_outer.astype(jnp.float32) * (filtered + skip_gain[None, :] * gated)
    local_squares = jnp.sum(conv_out * conv_out, axis=1)
    total_squares = lax.psum(local_squares, "chan")
    mean_square = total_squares / (width * chan_count)
    values = (conv_out * lax.rsqrt(mean_square[:, None] + 1e-06)).astype(jnp.bfloat16)
    score_scale = HD ** (-0.5)
    heads_here = width // HD
    my_start = seq_index * tok_rows
    all_pos = my_start + jnp.arange(tok_rows, dtype=jnp.int32)
    final_state = fold_keys(
        (
            jnp.full((heads_here, tok_rows), -1e30, jnp.float32),
            jnp.zeros((heads_here, tok_rows), jnp.float32),
            jnp.zeros((heads_here, tok_rows, HD), jnp.float32),
        ),
        query_rows,
        all_pos,
        (
            lax.all_gather(key_rows, "seq", axis=0, tiled=True),
            lax.all_gather(values, "seq", axis=0, tiled=True),
        ),
        score_scale,
    )
    mixed = finish(final_state)
    return mixed


def solution(mesh):
    in_specs = (
        P("seq", "chan"),
        P("seq", "chan"),
        P("seq", "chan"),
        P(None, "chan"),
        P(None, "chan"),
        P("chan"),
        P("seq", "chan"),
        P("seq", "chan"),
    )
    out_specs = P("seq", "chan")
    return jax.shard_map(local, mesh=mesh, in_specs=in_specs, out_specs=out_specs, check_vma=False)
```

profile of v0, /device:TPU:1, one launch (start us, length us, event | category | flops | bytes accessed | tf_op | source)
XLA Modules:
  0.0 426.7 jit_solution(17308309685470993890)
XLA Ops:
  6.5 0.7 copy.35
  7.3 1.0 convert_multiply_fusion
  8.5 1.6 copy.36
  10.2 1.6 fusion.21
  12.5 0.8 copy.26
  13.4 3.0 copy.37
  16.4 1.3 dynamic-slice
  17.7 0.7 dynamic-update-slice
  18.5 130.3 %all-reduce = f32[64]{0:T(128)S(1)} all-reduce(f32[64]{0:T(128)S(1)} %dynamic-update-slice), channel_id=1, replica_groups=mesh['seq'=64,'chan'=8] {'seq'}, use_global_device_ids=true, to_apply=%add | all-reduce | flops 64 | bytes 512
  148.8 2.0 while.30
  149.5 1.4 bitcast_add_fusion.3
  150.9 2.6 fusion.20
  153.7 16.0 %psum.7 = f32[128]{0:T(128)S(1)} all-reduce(f32[128]{0:T(128)S(1)} %multiply_reduce_fusion), channel_id=1, replica_groups=mesh['seq'=64,'chan'=8] {'chan'}, use_global_device_ids=true, to_apply=%region_4.5 | all-reduce | flops 128 | bytes 1024 | tf_op jit(solution)/shard_map/psum | solution.py:104
  169.7 0.7 multiply_convert_fusion
  170.5 21.5 %all-gather.5.cloned.1.call-done = bf16[8192,512]{0,1:T(8,128)(2,1)} async-done(((bf16[128,512]{0,1:T(8,128)(2,1)}), bf16[8192,512]{0,1:T(8,128)(2,1)}) %all-gather.5.cloned.1.call-update) | async-done | bytes 8388624 | tf_op jit(solution)/shard_map/all_gather | solution.py:120
  192.0 183.1 %all-gather.7.cloned.1.call-done = bf16[8192,512]{1,0:T(8,128)(2,1)} async-done(((bf16[128,512]{1,0:T(8,128)(2,1)}), bf16[8192,512]{1,0:T(8,128)(2,1)}) %all-gather.7.cloned.1.call-update) | async-done | bytes 8388624 | tf_op jit(solution)/shard_map/all_gather | solution.py:121
  375.1 44.3 %while.31 = (s32[]{:T(128)}, f32[4,128]{1,0:T(4,128)S(1)}, f32[4,128]{1,0:T(4,128)S(1)}, f32[4,128,128]{2,1,0:T(8,128)S(1)}, bf16[8192,512]{0,1:T(8,128)(2,1)}, ...) while((s32[]{:T(128)}, f32[4,128]{1,0:T(4,128)S(1)}, ...), condition=%wide.region_8.9_spmd.clone, body=%wide.region_5.8_spmd.clone.sunk | while | flops 275582592 | bytes 15901895 | solution.py:60
  375.3 1.3 constant_dynamic-slice_fusion.6
  377.2 1.3 constant_dynamic-slice_fusion.5
  378.5 0.6 fusion.46
  379.7 0.9 convolution_add_fusion.2
  380.9 1.3 constant_dynamic-slice_fusion.6
  382.7 1.3 constant_dynamic-slice_fusion.5
  384.0 0.6 fusion.46
  385.2 0.9 convolution_add_fusion.2
  386.4 1.3 constant_dynamic-slice_fusion.6
  388.2 1.3 constant_dynamic-slice_fusion.5
  389.5 0.6 fusion.46
  390.7 0.9 convolution_add_fusion.2
  391.9 1.3 constant_dynamic-slice_fusion.6
  393.8 1.3 constant_dynamic-slice_fusion.5
  395.1 0.6 fusion.46
  396.3 0.9 convolution_add_fusion.2
  397.5 1.3 constant_dynamic-slice_fusion.6
  399.3 1.3 constant_dynamic-slice_fusion.5
  400.6 0.6 fusion.46
  401.8 0.9 convolution_add_fusion.2
  403.0 1.3 constant_dynamic-slice_fusion.6
  404.9 1.3 constant_dynamic-slice_fusion.5
  407.4 0.9 convolution_add_fusion.2
  408.5 1.3 constant_dynamic-slice_fusion.6
  410.4 1.3 constant_dynamic-slice_fusion.5
  411.7 0.6 fusion.46
  412.9 0.9 convolution_add_fusion.2
  414.1 1.3 constant_dynamic-slice_fusion.6
  415.9 1.3 constant_dynamic-slice_fusion.5
  418.4 0.9 convolution_add_fusion.2
  419.4 0.8 copy_bitcast_fusion
  (103 shorter events, 13.7 us)
Async XLA Ops:
  6.5 142.3 %all-gather.9.cloned.1.call-start = ((), (), s32[]{:S(2)}) async-start(), calls=%async_computation.2 | async-start | bytes 1064960 | tf_op jit(solution)/shard_map/all_gather | solution.py:12
  10.2 1.7 copy-start.1
  10.2 2.3 copy-start.5
  12.5 179.6 %all-gather.5.cloned.1.call-start = ((), (), s32[]{:S(2)}) async-start(), calls=%async_computation | async-start | bytes 8519680 | tf_op jit(solution)/shard_map/all_gather | solution.py:120
  13.3 361.8 %all-gather.7.cloned.1.call-start = ((), (), s32[]{:S(2)}) async-start(), calls=%async_computation.1 | async-start | bytes 8519680 | tf_op jit(solution)/shard_map/all_gather | solution.py:121
  13.4 137.5 %copy-start.6 = (f32[8,512]{1,0:T(8,128)S(1)}, f32[8,512]{1,0:T(8,128)}, u32[]{:S(2)}) copy-start(f32[8,512]{1,0:T(8,128)} %param.16) | copy-start | bytes 49156
  16.4 137.1 %copy-start.2 = (bf16[128,512]{1,0:T(8,128)(2,1)S(1)}, bf16[128,512]{1,0:T(8,128)(2,1)}, u32[]{:S(2)}) copy-start(bf16[128,512]{1,0:T(8,128)(2,1)} %param.14) | copy-start | bytes 393220
  16.4 137.1 %copy-start.3 = (bf16[128,512]{1,0:T(8,128)(2,1)S(1)}, bf16[128,512]{1,0:T(8,128)(2,1)}, u32[]{:S(2)}) copy-start(bf16[128,512]{1,0:T(8,128)(2,1)} %param.13) | copy-start | bytes 393220
  16.4 137.1 %copy-start.4 = (bf16[128,512]{1,0:T(8,128)(2,1)S(1)}, bf16[128,512]{1,0:T(8,128)(2,1)}, u32[]{:S(2)}) copy-start(bf16[128,512]{1,0:T(8,128)(2,1)} %param.12) | copy-start | bytes 393220
  16.4 137.1 %copy-start.7 = (f32[512]{0:T(512)S(1)}, f32[512]{0:T(512)}, u32[]{:S(2)}) copy-start(f32[512]{0:T(512)} %param.17) | copy-start | bytes 6148
  150.9 224.2 %copy-start = (bf16[128,512]{1,0:T(8,128)(2,1)S(1)}, bf16[128,512]{1,0:T(8,128)(2,1)}, u32[]{:S(2)}) copy-start(bf16[128,512]{1,0:T(8,128)(2,1)} %param.18) | copy-start | bytes 393220
Sparse Core Ops, SparseCore 0:
  12.6 87.8 all-gather.8
  103.6 88.3 all-gather.4
  195.4 179.6 all-gather.6
where the time goes:
time: 433 us; the launch traced here: 427 us
  waiting for transfers between devices  205 us (47%)
  blocking collectives  146 us (34%)
  local copies, waits for them, and re-layouts  33.7 us (8%)
  other arithmetic  14.1 us (3%)
  matrix products  13.9 us (3%)
  between operations  13.3 us (3%)
    all_gather x1, waiting for transfers between devices, local(): lax.all_gather(values, 'seq', axis=0, tiled=True)  183 us
    unnamed x1, blocking collectives  130 us
    all_gather x1, waiting for transfers between devices, local(): lax.all_gather(key_rows, 'seq', axis=0, tiled=True)  21.5 us
    psum x1, blocking collectives, local(): total_squares = lax.psum(local_squares, 'chan')  16 us
    dynamic_slice x16, local copies, waits for them, and re-layouts, one_step(): value_part = lax.dynamic_slice_in_dim(value_piece, sub_start, step_rows, 0)  14.7 us
    dynamic_slice x8, local copies, waits for them, and re-layouts, one_step(): key_part = lax.dynamic_slice_in_dim(key_piece, sub_start, step_rows, 0)  10.4 us
  transfers between devices with their start and end apart: 3, of which 2 were waited for; matrix products, arithmetic and copies ran while one was open for 3% of the time, Pallas kernels for 0%

commit v1 on v0

--- a/solution.py
+++ b/solution.py
@@ -101,7 +101,10 @@
     filtered = jnp.sum(modal * (pole_weights * jnp.sqrt(pole_rates))[None, :, :], axis=1)
     conv_out = gate_outer.astype(jnp.float32) * (filtered + skip_gain[None, :] * gated)
     local_squares = jnp.sum(conv_out * conv_out, axis=1)
-    total_squares = lax.psum(local_squares, "chan")
+    size, total_squares = (lax.axis_size("chan"), local_squares)
+    for hop in [1 << k for k in range(size.bit_length() - 1)]:
+        swap = [(i, i ^ hop) for i in range(size)]
+        total_squares = total_squares + lax.ppermute(total_squares, "chan", swap)
     mean_square = total_squares / (width * chan_count)
     values = (conv_out * lax.rsqrt(mean_square[:, None] + 1e-06)).astype(jnp.bfloat16)
     score_scale = HD ** (-0.5)

time: 433 us -> 440 us (1.016)
  blocking collectives: 146 us -> 130 us
  waiting for transfers between devices: 205 us -> 218 us
  starting transfers between devices: 0.09 us -> 9.82 us
    psum x1 -> x0, blocking collectives: 16 us -> none  [local(): total_squares = lax.psum(local_squares, 'chan')]
    ppermute x0 -> x3, starting transfers between devices: none -> 9.74 us  [local(): total_squares = total_squares + lax.ppermute(total_squares, 'chan', swap)]
    ppermute x0 -> x3, waiting for transfers between devices: none -> 8.75 us  [local(): total_squares = total_squares + lax.ppermute(total_squares, 'chan', swap)]
    all_gather x1, waiting for transfers between devices: 183 us -> 189 us  [local(): lax.all_gather(values, 'seq', axis=0, tiled=True)]
  transfers between devices with their start and end apart: 3 -> 6, of which waited for: 2 -> 5; matrix products, arithmetic and copies ran while one was open for 3% -> 3% of each run, Pallas kernels for 0% -> 0%
where the time goes in v1:
time: 440 us; the launch traced here: 433 us
  waiting for transfers between devices  218 us (50%)
  blocking collectives  130 us (30%)
  local copies, waits for them, and re-layouts  33.6 us (8%)
  other arithmetic  14.1 us (3%)
  matrix products  13.9 us (3%)
  between operations  13.4 us (3%)
  starting transfers between devices  9.82 us (2%)
    all_gather x1, waiting for transfers between devices, local(): lax.all_gather(values, 'seq', axis=0, tiled=True)  189 us
    unnamed x1, blocking collectives  130 us
    all_gather x1, waiting for transfers between devices, local(): lax.all_gather(key_rows, 'seq', axis=0, tiled=True)  19.3 us
    dynamic_slice x16, local copies, waits for them, and re-layouts, one_step(): value_part = lax.dynamic_slice_in_dim(value_piece, sub_start, step_rows, 0)  14.7 us
    dynamic_slice x8, local copies, waits for them, and re-layouts, one_step(): key_part = lax.dynamic_slice_in_dim(key_piece, sub_start, step_rows, 0)  10.4 us
    ppermute x3, starting transfers between devices, local(): total_squares = total_squares + lax.ppermute(total_squares, 'chan', swap)  9.74 us
  transfers between devices with their start and end apart: 6, of which 5 were waited for; matrix products, arithmetic and copies ran while one was open for 3% of the time, Pallas kernels for 0%

profile of v1, /device:TPU:1, one launch (start us, length us, event | category | flops | bytes accessed | tf_op | source)
XLA Modules:
  0.0 433.3 jit_solution(5424454973071448094)
XLA Ops:
  6.5 0.7 copy.35
  7.3 1.0 convert_multiply_fusion
  8.5 1.6 copy.36
  10.2 1.6 fusion.21
  12.5 0.8 copy.26
  13.4 3.0 copy.37
  16.4 1.3 dynamic-slice
  17.7 0.7 dynamic-update-slice
  18.4 130.2 %all-reduce = f32[64]{0:T(128)S(1)} all-reduce(f32[64]{0:T(128)S(1)} %dynamic-update-slice), channel_id=1, replica_groups=mesh['seq'=64,'chan'=8] {'seq'}, use_global_device_ids=true, to_apply=%add | all-reduce | flops 64 | bytes 512
  148.7 2.0 while.30
  148.7 0.6 fusion.41
  149.3 1.4 bitcast_add_fusion.3
  150.7 2.6 fusion.20
  153.5 1.9 collective-permute-start
  155.5 2.8 collective-permute-done
  158.3 1.9 collective-permute-start.1
  160.2 3.7 collective-permute-done.1
  163.9 5.9 %collective-permute-start.2 = (f32[128]{0:T(128)S(1)}, f32[128]{0:T(128)S(1)}, u32[]{:S(2)}, u32[]{:S(2)}) collective-permute-start(f32[128]{0:T(128)S(1)} %add.109), channel_id=1, source_target_pairs={{0,4},{1,5},{2,6},{3,7},{4,0},{5,1},{6,2},{7,3},{8,12},{9,13},{10,... | collective-permute-start | bytes 1544 | tf_op jit(solution)/shard_map/ppermute | solution.py:107
  169.8 2.3 collective-permute-done.2
  172.1 0.8 multiply_convert_fusion
  172.9 19.3 %all-gather.5.cloned.1.call-done = bf16[8192,512]{0,1:T(8,128)(2,1)} async-done(((bf16[128,512]{0,1:T(8,128)(2,1)}), bf16[8192,512]{0,1:T(8,128)(2,1)}) %all-gather.5.cloned.1.call-update) | async-done | bytes 8388624 | tf_op jit(solution)/shard_map/all_gather | solution.py:123
  192.2 189.5 %all-gather.7.cloned.1.call-done = bf16[8192,512]{1,0:T(8,128)(2,1)} async-done(((bf16[128,512]{1,0:T(8,128)(2,1)}), bf16[8192,512]{1,0:T(8,128)(2,1)}) %all-gather.7.cloned.1.call-update) | async-done | bytes 8388624 | tf_op jit(solution)/shard_map/all_gather | solution.py:124
  381.7 44.3 %while.31 = (s32[]{:T(128)}, f32[4,128]{1,0:T(4,128)S(1)}, f32[4,128]{1,0:T(4,128)S(1)}, f32[4,128,128]{2,1,0:T(8,128)S(1)}, bf16[8192,512]{0,1:T(8,128)(2,1)}, ...) while((s32[]{:T(128)}, f32[4,128]{1,0:T(4,128)S(1)}, ...), condition=%wide.region_7.8_spmd.clone, body=%wide.region_4.7_spmd.clone.sunk | while | flops 275582592 | bytes 15901895 | solution.py:60
  381.9 1.3 constant_dynamic-slice_fusion.6
  383.8 1.3 constant_dynamic-slice_fusion.5
  386.3 0.9 convolution_add_fusion.2
  387.5 1.3 constant_dynamic-slice_fusion.6
  389.3 1.3 constant_dynamic-slice_fusion.5
  391.8 0.9 convolution_add_fusion.2
  393.0 1.3 constant_dynamic-slice_fusion.6
  394.9 1.3 constant_dynamic-slice_fusion.5
  397.4 0.9 convolution_add_fusion.2
  398.6 1.3 constant_dynamic-slice_fusion.6
  400.4 1.3 constant_dynamic-slice_fusion.5
  402.9 0.9 convolution_add_fusion.2
  404.1 1.3 constant_dynamic-slice_fusion.6
  405.9 1.3 constant_dynamic-slice_fusion.5
  408.4 0.9 convolution_add_fusion.2
  409.6 1.3 constant_dynamic-slice_fusion.6
  411.5 1.3 constant_dynamic-slice_fusion.5
  414.0 0.9 convolution_add_fusion.2
  415.2 1.3 constant_dynamic-slice_fusion.6
  417.0 1.3 constant_dynamic-slice_fusion.5
  419.5 0.9 convolution_add_fusion.2
  420.7 1.3 constant_dynamic-slice_fusion.6
  422.6 1.3 constant_dynamic-slice_fusion.5
  425.1 0.9 convolution_add_fusion.2
  426.0 0.8 copy_bitcast_fusion
  (110 shorter events, 16.9 us)
Async XLA Ops:
  6.5 142.1 %all-gather.9.cloned.1.call-start = ((), (), s32[]{:S(2)}) async-start(), calls=%async_computation.2 | async-start | bytes 1064960 | tf_op jit(solution)/shard_map/all_gather | solution.py:12
  10.2 1.7 copy-start.1
  10.2 2.3 copy-start.5
  12.5 179.8 %all-gather.5.cloned.1.call-start = ((), (), s32[]{:S(2)}) async-start(), calls=%async_computation | async-start | bytes 8519680 | tf_op jit(solution)/shard_map/all_gather | solution.py:123
  13.3 368.4 %all-gather.7.cloned.1.call-start = ((), (), s32[]{:S(2)}) async-start(), calls=%async_computation.1 | async-start | bytes 8519680 | tf_op jit(solution)/shard_map/all_gather | solution.py:124
  13.4 137.3 %copy-start.6 = (f32[8,512]{1,0:T(8,128)S(1)}, f32[8,512]{1,0:T(8,128)}, u32[]{:S(2)}) copy-start(f32[8,512]{1,0:T(8,128)} %param.16) | copy-start | bytes 49156
  16.4 137.0 %copy-start.2 = (bf16[128,512]{1,0:T(8,128)(2,1)S(1)}, bf16[128,512]{1,0:T(8,128)(2,1)}, u32[]{:S(2)}) copy-start(bf16[128,512]{1,0:T(8,128)(2,1)} %param.14) | copy-start | bytes 393220
  16.4 137.0 %copy-start.3 = (bf16[128,512]{1,0:T(8,128)(2,1)S(1)}, bf16[128,512]{1,0:T(8,128)(2,1)}, u32[]{:S(2)}) copy-start(bf16[128,512]{1,0:T(8,128)(2,1)} %param.13) | copy-start | bytes 393220
  16.4 137.0 %copy-start.4 = (bf16[128,512]{1,0:T(8,128)(2,1)S(1)}, bf16[128,512]{1,0:T(8,128)(2,1)}, u32[]{:S(2)}) copy-start(bf16[128,512]{1,0:T(8,128)(2,1)} %param.12) | copy-start | bytes 393220
  16.4 137.0 %copy-start.7 = (f32[512]{0:T(512)S(1)}, f32[512]{0:T(512)}, u32[]{:S(2)}) copy-start(f32[512]{0:T(512)} %param.17) | copy-start | bytes 6148
  150.7 231.0 %copy-start = (bf16[128,512]{1,0:T(8,128)(2,1)S(1)}, bf16[128,512]{1,0:T(8,128)(2,1)}, u32[]{:S(2)}) copy-start(bf16[128,512]{1,0:T(8,128)(2,1)} %param.18) | copy-start | bytes 393220
  153.5 4.7 %collective-permute-start = (f32[128]{0:T(128)S(1)}, f32[128]{0:T(128)S(1)}, u32[]{:S(2)}, u32[]{:S(2)}) collective-permute-start(f32[128]{0:T(128)S(1)} %multiply_reduce_fusion), channel_id=1, source_target_pairs={{0,1},{1,0},{2,3},{3,2},{4,5},{5,4},{6,7},{7,6},{8,9},{9,8},{10,11... | collective-permute-start | bytes 1544 | tf_op jit(solution)/shard_map/ppermute | solution.py:107
  158.3 5.6 %collective-permute-start.1 = (f32[128]{0:T(128)S(1)}, f32[128]{0:T(128)S(1)}, u32[]{:S(2)}, u32[]{:S(2)}) collective-permute-start(f32[128]{0:T(128)S(1)} %add.108), channel_id=1, source_target_pairs={{0,2},{1,3},{2,0},{3,1},{4,6},{5,7},{6,4},{7,5},{8,10},{9,11},{10,... | collective-permute-start | bytes 1544 | tf_op jit(solution)/shard_map/ppermute | solution.py:107
  163.9 8.2 %collective-permute-start.2 = (f32[128]{0:T(128)S(1)}, f32[128]{0:T(128)S(1)}, u32[]{:S(2)}, u32[]{:S(2)}) collective-permute-start(f32[128]{0:T(128)S(1)} %add.109), channel_id=1, source_target_pairs={{0,4},{1,5},{2,6},{3,7},{4,0},{5,1},{6,2},{7,3},{8,12},{9,13},{10,... | collective-permute-start | bytes 1544 | tf_op jit(solution)/shard_map/ppermute | solution.py:107
Sparse Core Ops, SparseCore 0:
  12.6 87.8 all-gather.8
  103.6 88.5 all-gather.4
  195.6 186.0 all-gather.6
